TPU v7x, 128 devices: a whole 4x4x4 slice. The times are simulated.
128 devices in a mesh: ep: 16 (over y, x_lo, core), edp: 8 (over z, x_hi).
Axes of the slice: x: 4 (x_hi: 2, x_lo: 2; x = x_hi * 2 + x_lo), y: 4, z: 4, core: 2. Of those that a mesh axis runs over, the one named last changes fastest.
Arguments:
- routed_hidden: bfloat16 [1, 16, 8192, 704], P(None, 'ep', 'edp'), may hold values from -6 to 6
- routed_grads: bfloat16 [1, 16, 8192, 2048], P(None, 'ep', 'edp'), may hold values from -6 to 6
- expert_counts: int32 [1, 8, 32], P(None, 'edp', 'ep'), may hold values from 1 to 512, as said below
- expert_offsets: int32 [1, 8, 32], P(None, 'edp', 'ep'), may hold values from 0 to 512, as said below
- attn_values: bfloat16 [1, 262144, 1024], P(None, ('ep', 'edp')), may hold values from -24 to 24
- attn_grads: bfloat16 [1, 262144, 2048], P(None, ('ep', 'edp')), may hold values from -6 to 6
- expert_master: float32 [1, 32, 704, 2048], P(None, 'ep', None, 'edp'), may hold values from -0.21875 to 0.21875
- expert_moment: float32 [1, 32, 704, 2048], P(None, 'ep', None, 'edp'), may hold values from -4 to 4
- expert_second: float32 [1, 32, 704, 2048], P(None, 'ep', None, 'edp'), may hold values from 0.1 to 2
- dense_master: float32 [1, 1024, 2048], P(None, ('ep', 'edp')), may hold values from -0.1875 to 0.1875
- dense_moment: float32 [1, 1024, 2048], P(None, ('ep', 'edp')), may hold values from -4 to 4
- dense_second: float32 [1, 1024, 2048], P(None, ('ep', 'edp')), may hold values from 0.1 to 2
Outputs:
- new_expert_master: float32 [1, 32, 704, 2048], P(None, 'ep', None, 'edp')
- new_expert_moment: float32 [1, 32, 704, 2048], P(None, 'ep', None, 'edp')
- new_expert_second: float32 [1, 32, 704, 2048], P(None, 'ep', None, 'edp')
- new_dense_master: float32 [1, 1024, 2048], P(None, ('ep', 'edp'))
- new_dense_moment: float32 [1, 1024, 2048], P(None, ('ep', 'edp'))
- new_dense_second: float32 [1, 1024, 2048], P(None, ('ep', 'edp'))
Inputs may be any that keep to these rules, and one draw needn't show every extreme that they name: `expert_counts`: in every layer, all 2 experts of some ep index in some buffer have count 512. `expert_offsets`: the segments of the 2 experts of one ep index in one buffer lie one after another in some order: the first placed starts at 0 and each next one starts at the previous start plus the previous count rounded up to a multiple of 128.
All inputs are finite; a program needn't handle non-finite values.
Results may differ from a plain program's by a relative error of at most 0.02.
Values may be sent and summed in bfloat16 or wider, within the bound.
A program may use at most 128 MiB of HBM per device.

v0:
```python
import jax
import jax.numpy as jnp
from jax import lax
from jax.sharding import PartitionSpec as P

D = 2048
FFW = 704
HW = 1024
LAYERS = 1
EXP_DEV = 2
CAP = 512


beta_one = 0.9
beta_two = 0.95
adam_step = 10.0
adam_eps = 1e-08
learn_rate = 0.01
decay_rate = 0.1


def adamw(master, moment, second, grad, factor):
    clipped = grad * factor
    new_moment = beta_one * moment + (1.0 - beta_one) * clipped
    new_second = beta_two * second + (1.0 - beta_two) * clipped * clipped
    corr_one = 1.0 - beta_one**adam_step
    corr_two = 1.0 - beta_two**adam_step
    update = (
        new_moment / corr_one / (jnp.sqrt(new_second / corr_two) + adam_eps) + decay_rate * master
    )
    return (master - learn_rate * update, new_moment, new_second)


def masked_grad(hidden_buf, grads_buf, row_count, row_start):
    hidden_win = lax.dynamic_slice_in_dim(hidden_buf, row_start, CAP, 0)
    grads_win = lax.dynamic_slice_in_dim(grads_buf, row_start, CAP, 0)
    row_keep = (jnp.arange(CAP, dtype=jnp.int32) < row_count).astype(hidden_win.dtype)
    return lax.dot_general(
        hidden_win * row_keep[:, None],
        grads_win,
        (((0,), (0,)), ((), ())),
        preferred_element_type=jnp.float32,
    )


def body(
    routed_hidden,
    routed_grads,
    expert_counts,
    expert_offsets,
    attn_values,
    attn_grads,
    expert_master,
    expert_moment,
    expert_second,
    dense_master,
    dense_moment,
    dense_second,
):
    layer_count = routed_hidden.shape[0]
    per_device = expert_counts.shape[2]
    partials = []
    hidden_buf = routed_hidden[0, 0]
    grads_buf = routed_grads[0, 0]
    for slot_idx in range(per_device):
        row_count = expert_counts[0, 0, slot_idx]
        row_start = expert_offsets[0, 0, slot_idx]
        partials.append(masked_grad(hidden_buf, grads_buf, row_count, row_start))
    stacked = jnp.stack(partials).reshape(
        layer_count, per_device, routed_hidden.shape[3], routed_grads.shape[3]
    )
    expert_total = lax.psum_scatter(
        stacked.astype(jnp.bfloat16), "edp", scatter_dimension=3, tiled=True
    ).astype(jnp.float32)
    dense_part = jnp.einsum(
        "ltf,ltd->lfd", attn_values, attn_grads, preferred_element_type=jnp.float32
    )
    dense_total = lax.psum_scatter(dense_part, ("ep", "edp"), scatter_dimension=1, tiled=True)
    expert_sq, dense_sq = lax.psum(
        (jnp.sum(expert_total * expert_total), jnp.sum(dense_total * dense_total)), ("ep", "edp")
    )
    total_count = float(LAYERS * EXP_DEV * lax.axis_size("ep") * FFW * D + LAYERS * HW * D)
    factor = jnp.minimum(1.0, jnp.sqrt(total_count) / (jnp.sqrt(expert_sq + dense_sq) + 1e-06))
    new_em, new_emo, new_es = adamw(
        expert_master, expert_moment, expert_second, expert_total, factor
    )
    new_dm, new_dmo, new_ds = adamw(dense_master, dense_moment, dense_second, dense_total, factor)
    return (new_em, new_emo, new_es, new_dm, new_dmo, new_ds)


def solution(mesh):
    return jax.shard_map(
        body,
        mesh=mesh,
        in_specs=(
            P(None, "ep", "edp", None),
            P(None, "ep", "edp", None),
            P(None, "edp", "ep"),
            P(None, "edp", "ep"),
            P(None, ("ep", "edp"), None),
            P(None, ("ep", "edp"), None),
            P(None, "ep", None, "edp"),
            P(None, "ep", None, "edp"),
            P(None, "ep", None, "edp"),
            P(None, ("ep", "edp"), None),
            P(None, ("ep", "edp"), None),
            P(None, ("ep", "edp"), None),
        ),
        out_specs=(
            P(None, "ep", None, "edp"),
            P(None, "ep", None, "edp"),
            P(None, "ep", None, "edp"),
            P(None, ("ep", "edp"), None),
            P(None, ("ep", "edp"), None),
            P(None, ("ep", "edp"), None),
        ),
        check_vma=False,
    )
```

profile of v0, /device:TPU:1, one launch (start us, length us, event | category | flops | bytes accessed | tf_op | source)
XLA Modules:
  0.0 858.2 jit_solution(12932337371781036616)
XLA Ops:
  7.2 0.0 reduce-scatter.3.cloned.1.call-start
  7.2 1.3 fusion.33
  11.1 1.3 fusion.32
  12.4 0.6 fusion.25
  13.1 0.7 fusion.26
  15.0 0.0 copy-start.5
  15.1 0.0 copy-start.6
  15.1 3.8 fusion.6
  18.9 0.0 copy-done.5
  18.9 0.0 copy-done.6
  18.9 1.8 fusion.7
  20.6 3.0 pad_maximum_fusion
  23.7 0.0 reduce-scatter.3.cloned.1.call-update
  23.7 0.0 reduce-scatter.5.cloned.1.call-start
  23.8 14.7 %fusion.2 = f32[1,1024,2048]{2,1,0:T(8,128)} fusion(bf16[1,2048,2048]{2,1,0:T(8,128)(2,1)} %param.17, bf16[1,2048,1024]{2,1,0:T(8,128)(2,1)} %param.16), kind=kOutput, calls=%fused_computation.3 | convolution fusion | flops 8589934592 | bytes 20971520 | tf_op jit(solution)/shard_map/ltf,ltd->lfd/dot_general | solution.py:75
  38.5 0.0 copy-start.2
  38.5 0.0 copy-start.3
  38.5 0.0 copy-start.4
  38.5 0.0 copy-start.1
  38.5 0.0 reduce-scatter.5.cloned.1.call-update
  38.6 83.0 %reduce-scatter.3.cloned.1.call-done = bf16[1,2,704,256]{3,2,1,0:T(8,128)(2,1)} async-done(((bf16[1,2,704,2048]{3,2,1,0:T(8,128)(2,1)}), bf16[1,2,704,256]{3,2,1,0:T(8,128)(2,1)}) %reduce-scatter.3.cloned.1.call-update) | async-done | bytes 720912 | tf_op jit(solution)/shard_map/reduce_scatter | solution.py:72
  121.5 0.0 copy-start
  121.5 2.2 fusion.14
  123.7 644.9 %reduce-scatter.5.cloned.1.call-done = f32[1,8,2048]{2,1,0:T(8,128)} async-done(((f32[1,1024,2048]{2,1,0:T(8,128)}), f32[1,8,2048]{2,1,0:T(8,128)}) %reduce-scatter.5.cloned.1.call-update) | async-done | bytes 65552 | tf_op jit(solution)/shard_map/reduce_scatter | solution.py:78
  768.5 1.5 multiply_reduce_fusion
  771.3 73.2 %psum.16 = f32[]{:T(128)} all-reduce(f32[]{:T(128)S(6)} %add.54), channel_id=1, replica_groups=mesh['ep'=16,'edp'=8] {'ep','edp'}, use_global_device_ids=true, to_apply=%region_2.0 | all-reduce | flops 1 | bytes 8 | tf_op jit(solution)/shard_map/psum | solution.py:79
  845.3 0.0 copy-done.2
  845.3 0.0 copy-done.3
  845.3 0.0 copy-done.4
  845.3 1.5 multiply_subtract_fusion.1
  846.8 0.0 copy-done.1
  846.8 0.0 copy-done
  846.8 4.6 multiply_subtract_fusion
Async XLA Ops:
  7.2 114.4 %reduce-scatter.3.cloned.1.call-start = ((), (), s32[]{:S(2)}) async-start(), calls=%async_computation.2 | async-start | bytes 6488064 | tf_op jit(solution)/shard_map/reduce_scatter | solution.py:72
  15.0 3.8 copy-start.5
  15.1 3.8 copy-start.6
  23.7 744.8 %reduce-scatter.5.cloned.1.call-start = ((), (), s32[]{:S(2)}) async-start(), calls=%async_computation.3 | async-start | bytes 8454144 | tf_op jit(solution)/shard_map/reduce_scatter | solution.py:78
  38.5 806.8 %copy-start.2 = (f32[1,8,2048]{2,1,0:T(8,128)S(1)}, f32[1,8,2048]{2,1,0:T(8,128)}, u32[]{:S(2)}) copy-start(f32[1,8,2048]{2,1,0:T(8,128)} %param.21) | copy-start | bytes 196612
  38.5 806.8 %copy-start.3 = (f32[1,8,2048]{2,1,0:T(8,128)S(1)}, f32[1,8,2048]{2,1,0:T(8,128)}, u32[]{:S(2)}) copy-start(f32[1,8,2048]{2,1,0:T(8,128)} %param.22) | copy-start | bytes 196612
  38.5 806.8 %copy-start.4 = (f32[1,8,2048]{2,1,0:T(8,128)S(1)}, f32[1,8,2048]{2,1,0:T(8,128)}, u32[]{:S(2)}) copy-start(f32[1,8,2048]{2,1,0:T(8,128)} %param.23) | copy-start | bytes 196612
  38.5 808.3 %copy-start.1 = (f32[1,2,704,256]{3,2,1,0:T(8,128)S(1)}, f32[1,2,704,256]{3,2,1,0:T(8,128)}, u32[]{:S(2)}) copy-start(f32[1,2,704,256]{3,2,1,0:T(8,128)} %param.18) | copy-start | bytes 4325380
  121.5 725.3 %copy-start = (bf16[1,2,704,256]{3,2,1,0:T(8,128)(2,1)S(1)}, bf16[1,2,704,256]{3,2,1,0:T(8,128)(2,1)}, u32[]{:S(2)}) copy-start(bf16[1,2,704,256]{3,2,1,0:T(8,128)(2,1)} %reduce-scatter.3.cloned.1.call-done) | copy-start | bytes 2162692
Sparse Core Ops, SparseCore 0:
  23.8 97.6 reduce-scatter.2
  123.9 644.5 reduce-scatter.4
where the time goes:
time: 859 us; the launch traced here: 858 us
  waiting for transfers between devices  728 us (85%)
  blocking collectives  73.2 us (9%)
  matrix products  20.3 us (2%)
  between operations  20.1 us (2%)
  other arithmetic  14.1 us (2%)
    reduce_scatter x1, waiting for transfers between devices, body(): lax.psum_scatter(dense_part, ('ep', 'edp'), scatter_dimension=1, tiled=True)  645 us
    reduce_scatter x1, waiting for transfers between devices, body(): lax.psum_scatter(stacked.astype(jnp.bfloat16), 'edp', scatter_dimension=3...  83 us
    psum x1, blocking collectives, body(): lax.psum((jnp.sum(expert_total * expert_total), jnp.sum(dense_total * den...  73.2 us
  transfers between devices with their start and end apart: 2, of which 2 were waited for; matrix products, arithmetic and copies ran while one was open for 2% of the time, Pallas kernels for 0%

commit v1 on v0

v1 whole, which is shorter than its diff:
```python
import jax
import jax.numpy as jnp
from jax import lax
from jax.experimental import pallas as pl
from jax.experimental.pallas import tpu as pltpu
from jax.sharding import PartitionSpec as P

D = 2048
FFW = 704
HW = 1024
LAYERS = 1
EXP_DEV = 2
HALF = FFW // 2
NCOL = 2
WCOL = D // NCOL

beta_one = 0.9
beta_two = 0.95
adam_step = 10.0
adam_eps = 1e-08
learn_rate = 0.01
decay_rate = 0.1

MESH = pl.DeviceIdType.MESH
TRANS = (((0,), (0,)), ((), ()))


def adamw(master, moment, second, grad, factor):
    clipped = grad * factor
    new_moment = beta_one * moment + (1.0 - beta_one) * clipped
    new_second = beta_two * second + (1.0 - beta_two) * clipped * clipped
    corr_one = 1.0 - beta_one**adam_step
    corr_two = 1.0 - beta_two**adam_step
    update = (
        new_moment / corr_one / (jnp.sqrt(new_second / corr_two) + adam_eps) + decay_rate * master
    )
    return (master - learn_rate * update, new_moment, new_second)


def grad_kernel(
    total_count,
    counts,
    offsets,
    hid_hbm,
    grd_hbm,
    val_hbm,
    att_hbm,
    exp_out,
    den_out,
    fac_out,
    hid,
    grd,
    val,
    att,
    hmask,
    part_a,
    part_b,
    recv_bx,
    fwd_a,
    cmb_a,
    dir_a,
    send_ax,
    recv_ax,
    fwd_b,
    cmb_b,
    dir_b,
    part_d,
    acc_d,
    fwd_y,
    cmb_y,
    dir_y,
    fwd_z,
    cmb_z,
    dir_z,
    recv_dx,
    sq_own,
    sq_row,
    recv_n1,
    recv_n2,
    load_sem,
    send_sem,
    recv_sem,
):
    ep = lax.axis_index("ep")
    edp = lax.axis_index("edp")
    y = ep // 4
    xl = (ep // 2) % 2
    core = ep % 2
    z = edp // 2
    xh = edp % 2
    x = xh * 2 + xl

    def dev(px, py, pz, pc):
        return (py * 4 + (px % 2) * 2 + pc, pz * 2 + px // 2)

    sibling = dev(x, y, z, 1 - core)
    z_next = dev(x, y, (z + 1) % 4, core)
    z_prev = dev(x, y, (z + 3) % 4, core)
    y_next = dev(x, (y + 1) % 4, z, core)
    y_prev = dev(x, (y + 3) % 4, z, core)

    loads = []
    for i, (src, dst) in enumerate(
        ((hid_hbm, hid), (grd_hbm, grd), (att_hbm, att), (val_hbm, val))
    ):
        loads.append(pltpu.make_async_copy(src, dst, load_sem.at[i]))
        loads[-1].start()

    barrier = pltpu.get_barrier_semaphore()
    ep_peers = [((ep + k) % 16, edp) for k in range(1, 16)]
    edp_peers = [(ep, (edp + k) % 8) for k in range(1, 8)]
    x_other = [dev((1 - xh) * 2 + 1 - xl, y, z, core)]
    greeted = ep_peers + edp_peers + x_other
    for peer in greeted:
        pl.semaphore_signal(barrier, inc=1, device_id=peer, device_id_type=MESH)

    loads[0].wait()
    lane = lax.broadcasted_iota(jnp.int32, (FFW, 1024), 1)
    for e in range(EXP_DEV):
        rel = lane - offsets[e]
        keep = jnp.logical_and(rel >= 0, rel < counts[e])
        hmask[e] = jnp.where(keep, hid[...], jnp.zeros_like(hid))
    loads[1].wait()

    started = []
    free = iter(range(200))

    def copy(src, dst, peer):
        i = next(free)
        return pltpu.make_async_remote_copy(
            src_ref=src,
            dst_ref=dst,
            send_sem=send_sem.at[i],
            recv_sem=recv_sem.at[i],
            device_id=peer,
            device_id_type=MESH,
        )

    def go(c):
        c.start()
        started.append(c)

    class Ring:
        def __init__(self, nxt, prv, block, fwd, cmb, direct, add):
            self.block, self.fwd, self.cmb, self.direct, self.add = block, fwd, cmb, direct, add
            self.fwd_copy = [copy(block(2, 0), fwd(0), nxt), copy(block(2, 1), fwd(1), prv)]
            self.dir_copy = [copy(block(1, 1), direct(0), nxt), copy(block(3, 0), direct(1), prv)]
            self.cmb_copy = [copy(fwd(0), cmb(0), nxt), copy(fwd(1), cmb(1), prv)]

        def send_far(self):
            for c in self.fwd_copy:
                go(c)

        def send_near(self, d):
            go(self.dir_copy[d])

        def relay(self):
            for d in (0, 1):
                self.fwd_copy[d].wait_recv()
                self.add(self.fwd(d), [self.fwd(d), self.block((1, 3)[d], d)])
                go(self.cmb_copy[d])

        def wait(self):
            for c in self.cmb_copy + self.dir_copy:
                c.wait_recv()

        def terms(self, h):
            return [self.block(0, h), self.cmb(h), self.direct(1 - h)]

    def add_bf16(dst, srcs):
        rows = 32

        def step(i, carry):
            r = pl.ds(pl.multiple_of(i * rows, rows), rows)
            total = srcs[0][r, :].astype(jnp.float32)
            for s in srcs[1:]:
                total += s[r, :].astype(jnp.float32)
            dst[r, :] = total.astype(dst.dtype)
            return carry

        lax.fori_loop(0, dst.shape[0] // rows, step, 0)

    def add_f32(dst, srcs):
        rows = 8

        def step(i, carry):
            r = pl.ds(pl.multiple_of(i * rows, rows), rows)
            total = srcs[0][r, :]
            for s in srcs[1:]:
                total += s[r, :]
            dst[r, :] = total
            return carry

        lax.fori_loop(0, dst.shape[0] // rows, step, 0)

    x_far = dev((x + 2) % 4, y, z, core)
    ring_a = Ring(
        z_next,
        z_prev,
        lambda k, h: part_a.at[(z + k) % 4, pl.ds(h * HALF, HALF)],
        lambda d: fwd_a.at[d],
        lambda d: cmb_a.at[d],
        lambda d: dir_a.at[d],
        add_bf16,
    )
    ring_b = Ring(
        z_next,
        z_prev,
        lambda k, h: part_b.at[xh, (z + k) % 4, pl.ds(h * HALF, HALF)],
        lambda d: fwd_b.at[d],
        lambda d: cmb_b.at[d],
        lambda d: dir_b.at[d],
        add_bf16,
    )
    ax_copy = copy(send_ax, recv_ax, x_far)
    bx_copy = {
        k: copy(part_b.at[1 - xh, (z + k) % 4], recv_bx.at[(z + k) % 4], x_far)
        for k in (2, 1, 3, 0)
    }

    def expert_part(k):
        c = (z + k) % 4
        cols = pl.ds(pl.multiple_of(c * 512, 512), 512)
        for e in (1, 0):
            prod = jnp.dot(
                hmask[e], grd[:, cols], preferred_element_type=jnp.float32
            ).astype(jnp.bfloat16)
            if e == 0:
                part_a[c] = prod
            else:
                part_b[0, c] = prod[:, :256]
                part_b[1, c] = prod[:, 256:]
                if k == 2:
                    pl.semaphore_wait(barrier, len(greeted))
                go(bx_copy[k])

    expert_part(2)
    ring_a.send_far()
    expert_part(1)
    expert_part(3)
    ring_a.send_near(0)
    ring_a.send_near(1)
    expert_part(0)

    def cols_of(n):
        return pl.ds(n * WCOL, WCOL)

    d0_copy = {}
    ring_y, ring_z, dx_copy = [], [], []
    for n in range(NCOL):
        for k in range(4):
            c = (y + k) % 4
            d0_copy[k, n] = copy(
                part_d.at[c, :, 1 - core, :, cols_of(n)], acc_d.at[c, :, :, cols_of(n)], sibling
            )
        ring_y.append(
            Ring(
                y_next,
                y_prev,
                lambda k, h, n=n: acc_d.at[(y + k) % 4, h, :, cols_of(n)],
                lambda d, n=n: fwd_y.at[n, d],
                lambda d, n=n: cmb_y.at[n, d],
                lambda d, n=n: dir_y.at[n, d],
                add_f32,
            )
        )
        ring_z.append(
            Ring(
                z_next,
                z_prev,
                lambda k, h, n=n: acc_d.at[
                    y, h, pl.ds(pl.multiple_of((z + k) % 4 * 16, 16), 16), cols_of(n)
                ],
                lambda d, n=n: fwd_z.at[n, d],
                lambda d, n=n: cmb_z.at[n, d],
                lambda d, n=n: dir_z.at[n, d],
                add_f32,
            )
        )

        def x_block(k, n=n):
            t = (x + k) % 4
            r = pl.multiple_of(z * 16 + t // 2 * 8, 8)
            return acc_d.at[y, t % 2, pl.ds(r, 8), cols_of(n)]

        dx_copy.append(
            [copy(x_block(k), recv_dx.at[n, k - 1], dev((x + k) % 4, y, z, core)) for k in (1, 2, 3)]
        )

    def dense_part(k):
        c = (y + k) % 4
        lhs = val[:, pl.ds(pl.multiple_of(c * 256, 256), 256)]
        for n in range(NCOL):
            prod = lax.dot_general(lhs, att[:, cols_of(n)], TRANS, preferred_element_type=jnp.float32)
            part_d[c, :, :, :, cols_of(n)] = prod.reshape(2, 2, 64, WCOL)
            go(d0_copy[k, n])

    def dense_core_sum(k):
        c = (y + k) % 4
        for n in range(NCOL):
            d0_copy[k, n].wait_recv()
            for h in (0, 1):
                mine = acc_d.at[c, h, :, cols_of(n)]
                add_f32(mine, [mine, part_d.at[c, h, core, :, cols_of(n)]])
            if k == 2:
                ring_y[n].send_far()
            elif k == 1:
                ring_y[n].send_near(0)
            elif k == 3:
                ring_y[n].send_near(1)

    def fold_b(k):
        bx_copy[k].wait_recv()
        c = (z + k) % 4
        mine = part_b.at[xh, c]
        add_bf16(mine, [mine, recv_bx.at[c]])

    loads[2].wait()
    loads[3].wait()
    dense_part(2)
    dense_part(1)
    dense_core_sum(2)
    dense_part(3)
    dense_core_sum(1)
    fold_b(2)
    ring_b.send_far()
    dense_part(0)
    dense_core_sum(3)
    dense_core_sum(0)
    ring_a.relay()
    fold_b(1)
    ring_b.send_near(0)
    fold_b(3)
    ring_b.send_near(1)
    ring_y[0].relay()
    ring_b.relay()
    ring_y[1].relay()

    ring_a.wait()
    own = pl.ds(pl.multiple_of(xh * 256, 256), 256)
    far = pl.ds(pl.multiple_of((1 - xh) * 256, 256), 256)
    for h in (0, 1):
        terms = ring_a.terms(h)

        def step_a(i, carry, h=h, terms=terms):
            r = pl.ds(pl.multiple_of(i * 32, 32), 32)
            o = pl.ds(pl.multiple_of(h * HALF + i * 32, 32), 32)
            send = sum(t[r, far].astype(jnp.float32) for t in terms)
            send_ax[o, :] = send.astype(jnp.bfloat16)
            exp_out[0, o, :] = sum(t[r, own].astype(jnp.float32) for t in terms)
            return carry

        lax.fori_loop(0, HALF // 32, step_a, 0)
    go(ax_copy)

    def dense_y_done(n):
        ring_y[n].wait()
        for h in (0, 1):
            terms = ring_y[n].terms(h)
            add_f32(terms[0], terms)
        ring_z[n].send_far()
        ring_z[n].send_near(0)
        ring_z[n].send_near(1)

    def dense_z_done(n):
        ring_z[n].wait()
        for h in (0, 1):
            terms = ring_z[n].terms(h)
            add_f32(terms[0], terms)
        for c in dx_copy[n]:
            go(c)

    dense_y_done(0)

    fold_b(0)
    ring_b.wait()
    squares = jnp.zeros((32, 256), jnp.float32)
    for h in (0, 1):
        terms = ring_b.terms(h)

        def step_b(i, sq, h=h, terms=terms):
            r = pl.ds(pl.multiple_of(i * 32, 32), 32)
            o = pl.ds(pl.multiple_of(h * HALF + i * 32, 32), 32)
            total = sum(t[r, :].astype(jnp.float32) for t in terms)
            exp_out[1, o, :] = total
            return sq + total * total

        squares = lax.fori_loop(0, HALF // 32, step_b, squares)

    ring_z[0].relay()
    dense_y_done(1)
    dense_z_done(0)

    ax_copy.wait_recv()

    def step_c(i, sq):
        r = pl.ds(pl.multiple_of(i * 32, 32), 32)
        total = exp_out[0, r, :] + recv_ax[r, :].astype(jnp.float32)
        exp_out[0, r, :] = total
        return sq + total * total

    squares = lax.fori_loop(0, FFW // 32, step_c, squares)
    tile = squares[:, :128] + squares[:, 128:]
    tile = tile[0:8] + tile[8:16] + tile[16:24] + tile[24:32]

    ring_z[1].relay()
    dense_z_done(1)
    for n in range(NCOL):
        for c in dx_copy[n]:
            c.wait_recv()
        r = pl.multiple_of(z * 16 + xh * 8, 8)
        total = acc_d[y, xl, pl.ds(r, 8), cols_of(n)]
        for k in range(3):
            total = total + recv_dx[n, k]
        den_out[:, cols_of(n)] = total
        sq = total * total
        for j in range(WCOL // 128):
            tile = tile + sq[:, j * 128 : (j + 1) * 128]

    sq_own[...] = tile
    n1 = [copy(sq_own, recv_n1.at[k], edp_peers[k]) for k in range(7)]
    for c in n1:
        go(c)
    for k, c in enumerate(n1):
        c.wait_recv()
        tile = tile + recv_n1[k]
    sq_row[...] = tile
    n2 = [copy(sq_row, recv_n2.at[k], ep_peers[k]) for k in range(15)]
    for c in n2:
        go(c)
    for k, c in enumerate(n2):
        c.wait_recv()
        tile = tile + recv_n2[k]
    norm = jnp.sqrt(jnp.sum(jnp.sum(tile, axis=0, keepdims=True), axis=1, keepdims=True))
    factor = jnp.minimum(1.0, jnp.sqrt(jnp.full((1, 1), total_count, jnp.float32)) / (norm + 1e-06))
    fac_out[...] = jnp.broadcast_to(factor, (8, 128))

    for c in started:
        c.wait_send()


def summed_grads(hid_t, grd, counts, offsets, val, att, total_count):
    vm = pltpu.VMEM
    bf = jnp.bfloat16
    f32 = jnp.float32
    hbm = pl.BlockSpec(memory_space=pl.ANY)
    smem = pl.BlockSpec(memory_space=pltpu.SMEM)
    vmem = pl.BlockSpec(memory_space=pltpu.VMEM)
    return pl.pallas_call(
        lambda *refs: grad_kernel(total_count, *refs),
        name="summed_grads",
        out_shape=(
            jax.ShapeDtypeStruct((2, FFW, 256), f32),
            jax.ShapeDtypeStruct((8, D), f32),
            jax.ShapeDtypeStruct((8, 128), f32),
        ),
        in_specs=[smem, smem, hbm, hbm, hbm, hbm],
        out_specs=(vmem, vmem, vmem),
        scratch_shapes=[
            vm((FFW, 1024), bf),
            vm((1024, D), bf),
            vm((2048, HW), bf),
            vm((2048, D), bf),
            vm((2, FFW, 1024), bf),
            vm((4, FFW, 512), bf),
            vm((2, 4, FFW, 256), bf),
            vm((4, FFW, 256), bf),
            vm((2, HALF, 512), bf),
            vm((2, HALF, 512), bf),
            vm((2, HALF, 512), bf),
            vm((FFW, 256), bf),
            vm((FFW, 256), bf),
            vm((2, HALF, 256), bf),
            vm((2, HALF, 256), bf),
            vm((2, HALF, 256), bf),
            vm((4, 2, 2, 64, D), f32),
            vm((4, 2, 64, D), f32),
            vm((NCOL, 2, 64, WCOL), f32),
            vm((NCOL, 2, 64, WCOL), f32),
            vm((NCOL, 2, 64, WCOL), f32),
            vm((NCOL, 2, 16, WCOL), f32),
            vm((NCOL, 2, 16, WCOL), f32),
            vm((NCOL, 2, 16, WCOL), f32),
            vm((NCOL, 3, 8, WCOL), f32),
            vm((8, 128), f32),
            vm((8, 128), f32),
            vm((7, 8, 128), f32),
            vm((15, 8, 128), f32),
            pltpu.SemaphoreType.DMA((4,)),
            pltpu.SemaphoreType.DMA((96,)),
            pltpu.SemaphoreType.DMA((96,)),
        ],
        compiler_params=pltpu.CompilerParams(
            collective_id=0, has_side_effects=True, vmem_limit_bytes=60 << 20
        ),
    )(counts, offsets, hid_t, grd, val, att)


def body(
    routed_hidden,
    routed_grads,
    expert_counts,
    expert_offsets,
    attn_values,
    attn_grads,
    expert_master,
    expert_moment,
    expert_second,
    dense_master,
    dense_moment,
    dense_second,
):
    total_count = float(LAYERS * EXP_DEV * lax.axis_size("ep") * FFW * D + LAYERS * HW * D)
    expert_total, dense_total, factor = summed_grads(
        routed_hidden[0, 0].T,
        routed_grads[0, 0],
        expert_counts[0, 0],
        expert_offsets[0, 0],
        attn_values[0],
        attn_grads[0],
        total_count,
    )
    factor = factor[0, 0]
    new_em, new_emo, new_es = adamw(
        expert_master, expert_moment, expert_second, expert_total[None], factor
    )
    new_dm, new_dmo, new_ds = adamw(
        dense_master, dense_moment, dense_second, dense_total[None], factor
    )
    return (new_em, new_emo, new_es, new_dm, new_dmo, new_ds)


def solution(mesh):
    return jax.shard_map(
        body,
        mesh=mesh,
        in_specs=(
            P(None, "ep", "edp", None),
            P(None, "ep", "edp", None),
            P(None, "edp", "ep"),
            P(None, "edp", "ep"),
            P(None, ("ep", "edp"), None),
            P(None, ("ep", "edp"), None),
            P(None, "ep", None, "edp"),
            P(None, "ep", None, "edp"),
            P(None, "ep", None, "edp"),
            P(None, ("ep", "edp"), None),
            P(None, ("ep", "edp"), None),
            P(None, ("ep", "edp"), None),
        ),
        out_specs=(
            P(None, "ep", None, "edp"),
            P(None, "ep", None, "edp"),
            P(None, "ep", None, "edp"),
            P(None, ("ep", "edp"), None),
            P(None, ("ep", "edp"), None),
            P(None, ("ep", "edp"), None),
        ),
        check_vma=False,
    )
```

time: 859 us -> 89.9 us (0.10)
  waiting for transfers between devices: 728 us -> 0 us
  Pallas kernels: 0 us -> 81.2 us
  blocking collectives: 73.2 us -> 0 us
  matrix products: 20.3 us -> 0 us
  between operations: 20.1 us -> 0.7 us
    reduce_scatter x2 -> x0, waiting for transfers between devices: 728 us -> none  [the longest x1 645 us: body(): lax.psum_scatter(dense_part, ('ep', 'edp'), scatter_dimension=1, tiled=True)]
    pallas_call x0 -> x1, Pallas kernels: none -> 81.2 us  [summed_grads(): pl.pallas_call(lambda *refs: grad_kernel(total_count, *refs), name='summe...]
    psum x1 -> x0, blocking collectives: 73.2 us -> none  [body(): lax.psum((jnp.sum(expert_total * expert_total), jnp.sum(dense_total * den...]
    dot_general x3 -> x0, matrix products: 20.3 us -> none  [the longest x1 14.7 us: body(): jnp.einsum('ltf,ltd->lfd', attn_values, attn_grads, preferred_element_typ...]
  transfers between devices with their start and end apart: 2 -> 0, of which waited for: 2 -> 0; matrix products, arithmetic and copies ran while one was open for 2% -> 0% of each run, Pallas kernels for 0% -> 0%
where the time goes in v1:
time: 89.9 us; the launch traced here: 89.7 us
  Pallas kernels  81.2 us (90%)
  other arithmetic  6.55 us (7%)
  local copies, waits for them, and re-layouts  1.24 us (1%)
    pallas_call x1, Pallas kernels, summed_grads(): pl.pallas_call(lambda *refs: grad_kernel(total_count, *refs), name='summe...  81.2 us
    sub x2, other arithmetic, adamw(): return (master - learn_rate * update, new_moment, new_second)  6.55 us

profile of v1, /device:TPU:1, one launch (start us, length us, event | category | flops | bytes accessed | tf_op | source)
XLA Modules:
  0.0 89.7 jit_solution(18321327632655420143)
XLA Ops:
  0.6 0.0 copy-start
  0.6 0.0 copy-start.1
  0.7 81.2 %summed_grads.1 = (f32[2,704,256]{2,1,0:T(8,128)}, f32[8,2048]{1,0:T(8,128)}, f32[8,128]{1,0:T(8,128)}) custom-call(s32[2]{0:T(128)} %bitcast.29, s32[2]{0:T(128)} %bitcast.30, bf16[704,1024]{1,0:T(8,128)(2,1)} %bitcast.28, bf16[1024,2048]{1,0:T(8,128)(2,1)} %bitcast.26, bf16[2048,1024]{1,0:T(8,128)(2,1)} %bitcast.27, bf16[2048,2048]{1,0:T(8,128)(2,1)} %bitcast.25), custom_call_target="tpu_custom_call" | custom-call | tf_op jit(solution)/shard_map/summed_grads/pallas_call | solution.py:449
  81.9 1.2 %slice.3 = f32[1,1]{1,0:T(1,128)} slice(f32[8,128]{1,0:T(8,128)} %get-tuple-element.10), slice={[0:1], [0:1]} | slice | bytes 8 | tf_op jit(solution)/shard_map/slice | solution.py:523
  83.1 0.0 copy-done
  83.1 0.0 copy-done.1
  83.1 0.0 copy-start.2
  83.1 0.0 copy-start.3
  83.1 0.0 copy-start.4
  83.1 0.0 copy-start.5
  83.1 5.2 %multiply_subtract_fusion = (f32[1,2,704,256]{3,2,1,0:T(8,128)}, f32[1,2,704,256]{3,2,1,0:T(8,128)}, f32[1,2,704,256]{3,2,1,0:T(8,128)}) fusion(f32[1,2,704,256]{3,2,1,0:T(8,128)S(1)} %copy-done, f32[2,704,256]{2,1,0:T(8,128)} %get-tuple-element.9, f32[]{:T(128)} %bitcast.7, f32[1,2,704,256]{3,2,1,0:T(8,128)S(1)} %copy-done.1, f32[1,2,704,256]{3,2,1,0:T(8,128)} %param.20), kind=kLoop, calls=%fused_computation.4 | loop fusion | flops 5767168 | bytes 10092548 | tf_op jit(solution)/shard_map/sub | solution.py:37
  88.4 0.0 copy-done.2
  88.4 0.0 copy-done.3
  88.4 0.0 copy-done.4
  88.4 0.0 copy-done.5
  88.4 1.3 %multiply_subtract_fusion.1 = (f32[1,8,2048]{2,1,0:T(8,128)}, f32[1,8,2048]{2,1,0:T(8,128)}, f32[1,8,2048]{2,1,0:T(8,128)}) fusion(f32[1,8,2048]{2,1,0:T(8,128)S(1)} %copy-done.2, f32[8,2048]{1,0:T(8,128)S(1)} %copy-done.5, f32[]{:T(128)} %bitcast.7, f32[1,8,2048]{2,1,0:T(8,128)S(1)} %copy-done.3, f32[1,8,2048]{2,1,0:T(8,128)S(1)} %copy-done.4), kind=kLoop, calls=%fused_computation.9 | loop fusion | flops 262144 | bytes 458756 | tf_op jit(solution)/shard_map/sub | solution.py:37
Async XLA Ops:
  0.6 82.5 %copy-start = (f32[1,2,704,256]{3,2,1,0:T(8,128)S(1)}, f32[1,2,704,256]{3,2,1,0:T(8,128)}, u32[]{:S(2)}) copy-start(f32[1,2,704,256]{3,2,1,0:T(8,128)} %param.18) | copy-start | bytes 4325380
  0.6 82.5 %copy-start.1 = (f32[1,2,704,256]{3,2,1,0:T(8,128)S(1)}, f32[1,2,704,256]{3,2,1,0:T(8,128)}, u32[]{:S(2)}) copy-start(f32[1,2,704,256]{3,2,1,0:T(8,128)} %param.19) | copy-start | bytes 4325380
  83.1 5.3 %copy-start.2 = (f32[1,8,2048]{2,1,0:T(8,128)S(1)}, f32[1,8,2048]{2,1,0:T(8,128)}, u32[]{:S(2)}) copy-start(f32[1,8,2048]{2,1,0:T(8,128)} %param.21) | copy-start | bytes 196612
  83.1 5.3 %copy-start.3 = (f32[1,8,2048]{2,1,0:T(8,128)S(1)}, f32[1,8,2048]{2,1,0:T(8,128)}, u32[]{:S(2)}) copy-start(f32[1,8,2048]{2,1,0:T(8,128)} %param.22) | copy-start | bytes 196612
  83.1 5.3 %copy-start.4 = (f32[1,8,2048]{2,1,0:T(8,128)S(1)}, f32[1,8,2048]{2,1,0:T(8,128)}, u32[]{:S(2)}) copy-start(f32[1,8,2048]{2,1,0:T(8,128)} %param.23) | copy-start | bytes 196612
  83.1 5.3 %copy-start.5 = (f32[8,2048]{1,0:T(8,128)S(1)}, f32[8,2048]{1,0:T(8,128)}, u32[]{:S(2)}) copy-start(f32[8,2048]{1,0:T(8,128)} %get-tuple-element.11) | copy-start | bytes 196612

commit v2 on v1

--- a/solution.py
+++ b/solution.py
@@ -11,7 +11,7 @@
 LAYERS = 1
 EXP_DEV = 2
 HALF = FFW // 2
-NCOL = 2
+NCOL = 4
 WCOL = D // NCOL
 
 beta_one = 0.9
@@ -99,28 +99,48 @@
     y_next = dev(x, (y + 1) % 4, z, core)
     y_prev = dev(x, (y + 3) % 4, z, core)
 
-    loads = []
-    for i, (src, dst) in enumerate(
-        ((hid_hbm, hid), (grd_hbm, grd), (att_hbm, att), (val_hbm, val))
-    ):
-        loads.append(pltpu.make_async_copy(src, dst, load_sem.at[i]))
-        loads[-1].start()
-
     barrier = pltpu.get_barrier_semaphore()
     ep_peers = [((ep + k) % 16, edp) for k in range(1, 16)]
     edp_peers = [(ep, (edp + k) % 8) for k in range(1, 8)]
-    x_other = [dev((1 - xh) * 2 + 1 - xl, y, z, core)]
-    greeted = ep_peers + edp_peers + x_other
+    x_peers = [dev((x + k) % 4, y, z, core) for k in (1, 2, 3)]
+    greeted = [sibling, y_next, y_prev, z_next, z_prev] + x_peers
     for peer in greeted:
         pl.semaphore_signal(barrier, inc=1, device_id=peer, device_id_type=MESH)
 
-    loads[0].wait()
+    loads = {}
+
+    def load(key, src, dst):
+        loads[key] = pltpu.make_async_copy(src, dst, load_sem.at[len(loads)])
+        loads[key].start()
+
+    def load_columns(key, src, dst, start, width):
+        cols = pl.ds(pl.multiple_of(start, width), width)
+        load(key, src.at[:, cols], dst.at[:, cols])
+
+    load("hid", hid_hbm, hid)
+    load_columns(("grd", 2), grd_hbm, grd, (z + 2) % 4 * 512, 512)
+    load_columns(("val", 2), val_hbm, val, (y + 2) % 4 * 256, 256)
+    load_columns(("att", 0), att_hbm, att, 0, WCOL)
+    for k in (1, 3, 0):
+        load_columns(("val", k), val_hbm, val, (y + k) % 4 * 256, 256)
+        load_columns(("grd", k), grd_hbm, grd, (z + k) % 4 * 512, 512)
+        if k != 0:
+            load_columns(("att", (k + 1) // 2), att_hbm, att, (k + 1) // 2 * WCOL, WCOL)
+    load_columns(("att", 3), att_hbm, att, 3 * WCOL, WCOL)
+    used = set()
+
+    def loaded(*keys):
+        for key in keys:
+            if key not in used:
+                used.add(key)
+                loads[key].wait()
+
+    loaded("hid")
     lane = lax.broadcasted_iota(jnp.int32, (FFW, 1024), 1)
     for e in range(EXP_DEV):
         rel = lane - offsets[e]
         keep = jnp.logical_and(rel >= 0, rel < counts[e])
         hmask[e] = jnp.where(keep, hid[...], jnp.zeros_like(hid))
-    loads[1].wait()
 
     started = []
     free = iter(range(200))
@@ -136,9 +156,21 @@
             device_id_type=MESH,
         )
 
+    held = []
+
     def go(c):
-        c.start()
+        if held is not None:
+            held.append(c)
+        else:
+            c.start()
         started.append(c)
+
+    def enter():
+        nonlocal held
+        pl.semaphore_wait(barrier, len(greeted))
+        for c in held:
+            c.start()
+        held = None
 
     class Ring:
         def __init__(self, nxt, prv, block, fwd, cmb, direct, add):
@@ -181,7 +213,7 @@
         lax.fori_loop(0, dst.shape[0] // rows, step, 0)
 
     def add_f32(dst, srcs):
-        rows = 8
+        rows = 16
 
         def step(i, carry):
             r = pl.ds(pl.multiple_of(i * rows, rows), rows)
@@ -193,7 +225,7 @@
 
         lax.fori_loop(0, dst.shape[0] // rows, step, 0)
 
-    x_far = dev((x + 2) % 4, y, z, core)
+    x_far = x_peers[1]
     ring_a = Ring(
         z_next,
         z_prev,
@@ -221,6 +253,7 @@
     def expert_part(k):
         c = (z + k) % 4
         cols = pl.ds(pl.multiple_of(c * 512, 512), 512)
+        loaded(("grd", k))
         for e in (1, 0):
             prod = jnp.dot(
                 hmask[e], grd[:, cols], preferred_element_type=jnp.float32
@@ -230,17 +263,7 @@
             else:
                 part_b[0, c] = prod[:, :256]
                 part_b[1, c] = prod[:, 256:]
-                if k == 2:
-                    pl.semaphore_wait(barrier, len(greeted))
                 go(bx_copy[k])
-
-    expert_part(2)
-    ring_a.send_far()
-    expert_part(1)
-    expert_part(3)
-    ring_a.send_near(0)
-    ring_a.send_near(1)
-    expert_part(0)
 
     def cols_of(n):
         return pl.ds(n * WCOL, WCOL)
@@ -287,27 +310,26 @@
             [copy(x_block(k), recv_dx.at[n, k - 1], dev((x + k) % 4, y, z, core)) for k in (1, 2, 3)]
         )
 
-    def dense_part(k):
+    def dense_part(k, n):
         c = (y + k) % 4
+        loaded(("val", k), ("att", n))
         lhs = val[:, pl.ds(pl.multiple_of(c * 256, 256), 256)]
-        for n in range(NCOL):
-            prod = lax.dot_general(lhs, att[:, cols_of(n)], TRANS, preferred_element_type=jnp.float32)
-            part_d[c, :, :, :, cols_of(n)] = prod.reshape(2, 2, 64, WCOL)
-            go(d0_copy[k, n])
-
-    def dense_core_sum(k):
+        prod = lax.dot_general(lhs, att[:, cols_of(n)], TRANS, preferred_element_type=jnp.float32)
+        part_d[c, :, :, :, cols_of(n)] = prod.reshape(2, 2, 64, WCOL)
+        go(d0_copy[k, n])
+
+    def dense_core_sum(k, n):
         c = (y + k) % 4
-        for n in range(NCOL):
-            d0_copy[k, n].wait_recv()
-            for h in (0, 1):
-                mine = acc_d.at[c, h, :, cols_of(n)]
-                add_f32(mine, [mine, part_d.at[c, h, core, :, cols_of(n)]])
-            if k == 2:
-                ring_y[n].send_far()
-            elif k == 1:
-                ring_y[n].send_near(0)
-            elif k == 3:
-                ring_y[n].send_near(1)
+        d0_copy[k, n].wait_recv()
+        for h in (0, 1):
+            mine = acc_d.at[c, h, :, cols_of(n)]
+            add_f32(mine, [mine, part_d.at[c, h, core, :, cols_of(n)]])
+        if k == 2:
+            ring_y[n].send_far()
+        elif k == 1:
+            ring_y[n].send_near(0)
+        elif k == 3:
+            ring_y[n].send_near(1)
 
     def fold_b(k):
         bx_copy[k].wait_recv()
@@ -315,43 +337,24 @@
         mine = part_b.at[xh, c]
         add_bf16(mine, [mine, recv_bx.at[c]])
 
-    loads[2].wait()
-    loads[3].wait()
-    dense_part(2)
-    dense_part(1)
-    dense_core_sum(2)
-    dense_part(3)
-    dense_core_sum(1)
-    fold_b(2)
-    ring_b.send_far()
-    dense_part(0)
-    dense_core_sum(3)
-    dense_core_sum(0)
-    ring_a.relay()
-    fold_b(1)
-    ring_b.send_near(0)
-    fold_b(3)
-    ring_b.send_near(1)
-    ring_y[0].relay()
-    ring_b.relay()
-    ring_y[1].relay()
-
-    ring_a.wait()
     own = pl.ds(pl.multiple_of(xh * 256, 256), 256)
     far = pl.ds(pl.multiple_of((1 - xh) * 256, 256), 256)
-    for h in (0, 1):
-        terms = ring_a.terms(h)
-
-        def step_a(i, carry, h=h, terms=terms):
-            r = pl.ds(pl.multiple_of(i * 32, 32), 32)
-            o = pl.ds(pl.multiple_of(h * HALF + i * 32, 32), 32)
-            send = sum(t[r, far].astype(jnp.float32) for t in terms)
-            send_ax[o, :] = send.astype(jnp.bfloat16)
-            exp_out[0, o, :] = sum(t[r, own].astype(jnp.float32) for t in terms)
-            return carry
-
-        lax.fori_loop(0, HALF // 32, step_a, 0)
-    go(ax_copy)
+
+    def expert_a_done():
+        ring_a.wait()
+        for h in (0, 1):
+            terms = ring_a.terms(h)
+
+            def step_a(i, carry, h=h, terms=terms):
+                r = pl.ds(pl.multiple_of(i * 32, 32), 32)
+                o = pl.ds(pl.multiple_of(h * HALF + i * 32, 32), 32)
+                send = sum(t[r, far].astype(jnp.float32) for t in terms)
+                send_ax[o, :] = send.astype(jnp.bfloat16)
+                exp_out[0, o, :] = sum(t[r, own].astype(jnp.float32) for t in terms)
+                return carry
+
+            lax.fori_loop(0, HALF // 32, step_a, 0)
+        go(ax_copy)
 
     def dense_y_done(n):
         ring_y[n].wait()
@@ -370,42 +373,34 @@
         for c in dx_copy[n]:
             go(c)
 
-    dense_y_done(0)
-
-    fold_b(0)
-    ring_b.wait()
-    squares = jnp.zeros((32, 256), jnp.float32)
-    for h in (0, 1):
-        terms = ring_b.terms(h)
-
-        def step_b(i, sq, h=h, terms=terms):
+    sums = {"wide": jnp.zeros((32, 256), jnp.float32), "tile": jnp.zeros((8, 128), jnp.float32)}
+
+    def expert_b_done():
+        ring_b.wait()
+        for h in (0, 1):
+            terms = ring_b.terms(h)
+
+            def step_b(i, sq, h=h, terms=terms):
+                r = pl.ds(pl.multiple_of(i * 32, 32), 32)
+                o = pl.ds(pl.multiple_of(h * HALF + i * 32, 32), 32)
+                total = sum(t[r, :].astype(jnp.float32) for t in terms)
+                exp_out[1, o, :] = total
+                return sq + total * total
+
+            sums["wide"] = lax.fori_loop(0, HALF // 32, step_b, sums["wide"])
+
+    def expert_a_last():
+        ax_copy.wait_recv()
+
+        def step_c(i, sq):
             r = pl.ds(pl.multiple_of(i * 32, 32), 32)
-            o = pl.ds(pl.multiple_of(h * HALF + i * 32, 32), 32)
-            total = sum(t[r, :].astype(jnp.float32) for t in terms)
-            exp_out[1, o, :] = total
+            total = exp_out[0, r, :] + recv_ax[r, :].astype(jnp.float32)
+            exp_out[0, r, :] = total
             return sq + total * total
 
-        squares = lax.fori_loop(0, HALF // 32, step_b, squares)
-
-    ring_z[0].relay()
-    dense_y_done(1)
-    dense_z_done(0)
-
-    ax_copy.wait_recv()
-
-    def step_c(i, sq):
-        r = pl.ds(pl.multiple_of(i * 32, 32), 32)
-        total = exp_out[0, r, :] + recv_ax[r, :].astype(jnp.float32)
-        exp_out[0, r, :] = total
-        return sq + total * total
-
-    squares = lax.fori_loop(0, FFW // 32, step_c, squares)
-    tile = squares[:, :128] + squares[:, 128:]
-    tile = tile[0:8] + tile[8:16] + tile[16:24] + tile[24:32]
-
-    ring_z[1].relay()
-    dense_z_done(1)
-    for n in range(NCOL):
+        sums["wide"] = lax.fori_loop(0, FFW // 32, step_c, sums["wide"])
+
+    def dense_last(n):
         for c in dx_copy[n]:
             c.wait_recv()
         r = pl.multiple_of(z * 16 + xh * 8, 8)
@@ -415,8 +410,84 @@
         den_out[:, cols_of(n)] = total
         sq = total * total
         for j in range(WCOL // 128):
-            tile = tile + sq[:, j * 128 : (j + 1) * 128]
-
+            sums["tile"] = sums["tile"] + sq[:, j * 128 : (j + 1) * 128]
+
+    expert_part(2)
+    ring_a.send_far()
+    dense_part(2, 1)
+    dense_part(2, 0)
+    enter()
+    dense_part(3, 0)
+    expert_part(3)
+    dense_core_sum(2, 1)
+    dense_part(1, 1)
+    dense_part(3, 1)
+    dense_core_sum(2, 0)
+    ring_a.send_near(1)
+    dense_part(1, 0)
+    dense_core_sum(3, 1)
+    expert_part(1)
+    dense_core_sum(1, 0)
+    dense_part(2, 2)
+    ring_a.send_near(0)
+    dense_core_sum(1, 1)
+    dense_part(2, 3)
+    dense_part(1, 2)
+    dense_core_sum(3, 0)
+    dense_part(0, 0)
+    ring_y[1].relay()
+    fold_b(2)
+    dense_part(3, 3)
+    ring_a.relay()
+    dense_part(0, 1)
+    dense_part(3, 2)
+    ring_y[0].relay()
+    dense_part(1, 3)
+    dense_core_sum(2, 2)
+    dense_core_sum(0, 0)
+    dense_core_sum(1, 2)
+    ring_b.send_far()
+    expert_part(0)
+    dense_core_sum(3, 3)
+    dense_core_sum(2, 3)
+    dense_y_done(0)
+    dense_core_sum(3, 2)
+    dense_part(0, 3)
+    dense_core_sum(1, 3)
+    fold_b(1)
+    ring_y[2].relay()
+    dense_part(0, 2)
+    dense_core_sum(0, 1)
+    expert_a_done()
+    dense_core_sum(0, 2)
+    dense_y_done(1)
+    dense_core_sum(0, 3)
+    fold_b(3)
+    ring_y[3].relay()
+    ring_z[0].relay()
+    ring_b.relay()
+    dense_y_done(2)
+    dense_y_done(3)
+    ring_z[2].relay()
+    ring_z[1].relay()
+    ring_z[3].relay()
+    ring_b.send_near(0)
+    ring_b.send_near(1)
+    dense_z_done(0)
+    fold_b(0)
+    dense_z_done(2)
+    expert_a_last()
+    dense_z_done(1)
+    dense_z_done(3)
+    dense_last(1)
+    dense_last(0)
+    dense_last(2)
+    expert_b_done()
+    dense_last(3)
+
+    tile = sums["wide"][:, :128] + sums["wide"][:, 128:]
+    tile = sums["tile"] + tile[0:8] + tile[8:16] + tile[16:24] + tile[24:32]
+    tile = jnp.sum(tile, axis=0, keepdims=True)
     sq_own[...] = tile
     n1 = [copy(sq_own, recv_n1.at[k], edp_peers[k]) for k in range(7)]
     for c in n1:
@@ -431,7 +502,7 @@
     for k, c in enumerate(n2):
         c.wait_recv()
         tile = tile + recv_n2[k]
-    norm = jnp.sqrt(jnp.sum(jnp.sum(tile, axis=0, keepdims=True), axis=1, keepdims=True))
+    norm = jnp.sqrt(jnp.sum(tile, axis=1, keepdims=True))
     factor = jnp.minimum(1.0, jnp.sqrt(jnp.full((1, 1), total_count, jnp.float32)) / (norm + 1e-06))
     fac_out[...] = jnp.broadcast_to(factor, (8, 128))
 
@@ -443,7 +514,7 @@
     vm = pltpu.VMEM
     bf = jnp.bfloat16
     f32 = jnp.float32
-    hbm = pl.BlockSpec(memory_space=pl.ANY)
+    hbm = pl.BlockSpec(memory_space=pltpu.HBM)
     smem = pl.BlockSpec(memory_space=pltpu.SMEM)
     vmem = pl.BlockSpec(memory_space=pltpu.VMEM)
     return pl.pallas_call(
@@ -482,18 +553,61 @@
             vm((NCOL, 2, 16, WCOL), f32),
             vm((NCOL, 2, 16, WCOL), f32),
             vm((NCOL, 3, 8, WCOL), f32),
-            vm((8, 128), f32),
-            vm((8, 128), f32),
-            vm((7, 8, 128), f32),
-            vm((15, 8, 128), f32),
-            pltpu.SemaphoreType.DMA((4,)),
-            pltpu.SemaphoreType.DMA((96,)),
-            pltpu.SemaphoreType.DMA((96,)),
+            vm((1, 128), f32),
+            vm((1, 128), f32),
+            vm((7, 1, 128), f32),
+            vm((15, 1, 128), f32),
+            pltpu.SemaphoreType.DMA((13,)),
+            pltpu.SemaphoreType.DMA((115,)),
+            pltpu.SemaphoreType.DMA((115,)),
         ],
         compiler_params=pltpu.CompilerParams(
-            collective_id=0, has_side_effects=True, vmem_limit_bytes=60 << 20
+            collective_id=0, has_side_effects=True, vmem_limit_bytes=52 << 20
         ),
     )(counts, offsets, hid_t, grd, val, att)
+
+
+STEPS = 11
+
+
+def adam_kernel(fac, eg, ew, em, es, dg, dw, dm, ds, *rest):
+    outs, (ow, om, os_, pw, pm, ps), sem = rest[:6], rest[6:12], rest[12]
+    factor = fac[0:1, 0:1]
+    copies = []
+
+    def out(src, dst):
+        copies.append(pltpu.make_async_copy(src, dst, sem.at[len(copies)]))
+        copies[-1].start()
+
+    pw[...], pm[...], ps[...] = adamw(dw[...], dm[...], ds[...], dg[...], factor)
+    for src, dst in zip((pw, pm, ps), outs[3:]):
+        out(src, dst)
+    rows = EXP_DEV * FFW // STEPS
+    for i in range(STEPS):
+        r = pl.ds(i * rows, rows)
+        ow[r], om[r], os_[r] = adamw(ew[r], em[r], es[r], eg[r], factor)
+        for src, dst in zip((ow, om, os_), outs[:3]):
+            out(src.at[r], dst.at[r])
+    for c in copies:
+        c.wait()
+
+
+def updated(factor, expert, dense):
+    rows = EXP_DEV * FFW
+    vmem = pl.BlockSpec(memory_space=pltpu.VMEM)
+    hbm = pl.BlockSpec(memory_space=pl.ANY)
+    return pl.pallas_call(
+        adam_kernel,
+        name="clipped_adamw",
+        out_shape=[jax.ShapeDtypeStruct((rows, 256), jnp.float32)] * 3
+        + [jax.ShapeDtypeStruct((8, D), jnp.float32)] * 3,
+        in_specs=[vmem] * 9,
+        out_specs=[hbm] * 6,
+        scratch_shapes=[pltpu.VMEM((rows, 256), jnp.float32)] * 3
+        + [pltpu.VMEM((8, D), jnp.float32)] * 3
+        + [pltpu.SemaphoreType.DMA((3 * STEPS + 3,))],
+        compiler_params=pltpu.CompilerParams(vmem_limit_bytes=16 << 20),
+    )(factor, *expert, *dense)
 
 
 def body(
@@ -520,14 +634,15 @@
         attn_grads[0],
         total_count,
     )
-    factor = factor[0, 0]
-    new_em, new_emo, new_es = adamw(
-        expert_master, expert_moment, expert_second, expert_total[None], factor
+    expert = [
+        a.reshape(EXP_DEV * FFW, 256)
+        for a in (expert_total, expert_master, expert_moment, expert_second)
+    ]
+    dense = [a.reshape(8, D) for a in (dense_total, dense_master, dense_moment, dense_second)]
+    new = updated(factor, expert, dense)
+    return tuple(a.reshape(expert_master.shape) for a in new[:3]) + tuple(
+        a.reshape(dense_master.shape) for a in new[3:]
     )
-    new_dm, new_dmo, new_ds = adamw(
-        dense_master, dense_moment, dense_second, dense_total[None], factor
-    )
-    return (new_em, new_emo, new_es, new_dm, new_dmo, new_ds)
 
 
 def solution(mesh):

time: 89.9 us -> 77.5 us (0.86)
  other arithmetic: 6.55 us -> 0 us
  Pallas kernels: 81.2 us -> 75.1 us
    pallas_call x1, Pallas kernels: 81.2 us -> 72.1 us  [summed_grads(): pl.pallas_call(lambda *refs: grad_kernel(total_count, *refs), name='summe...]
    sub x2 -> x0, other arithmetic: 6.55 us -> none  [adamw(): return (master - learn_rate * update, new_moment, new_second)]
    pallas_call x0 -> x1, Pallas kernels: none -> 3.01 us  [updated(): pl.pallas_call(adam_kernel, name='clipped_adamw', out_shape=[jax.ShapeDty...]
    unnamed x12 -> x16, local copies, waits for them, and re-layouts: 0.03 us -> 1.33 us
    slice x1 -> x0, local copies, waits for them, and re-layouts: 1.21 us -> none  [body(): factor = factor[0, 0]]
where the time goes in v2:
time: 77.5 us; the launch traced here: 77.3 us
  Pallas kernels  75.1 us (97%)
  local copies, waits for them, and re-layouts  1.33 us (2%)
  between operations  0.9 us (1%)
    pallas_call x1, Pallas kernels, summed_grads(): pl.pallas_call(lambda *refs: grad_kernel(total_count, *refs), name='summe...  72.1 us
    pallas_call x1, Pallas kernels, updated(): pl.pallas_call(adam_kernel, name='clipped_adamw', out_shape=[jax.ShapeDty...  3.01 us

profile of v2, /device:TPU:1, one launch (start us, length us, event | category | flops | bytes accessed | tf_op | source)
XLA Modules:
  0.0 77.3 jit_solution(2894023463755194272)
XLA Ops:
  0.6 0.0 copy-start.6
  0.6 0.6 copy-done.6
  1.3 0.0 copy-start.7
  1.3 0.7 copy-done.7
  1.9 0.0 copy-start
  2.0 0.0 copy-start.1
  2.0 0.0 copy-start.2
  2.0 0.0 copy-start.3
  2.0 0.0 copy-start.4
  2.0 0.0 copy-start.5
  2.0 72.1 %summed_grads.1 = (f32[2,704,256]{2,1,0:T(8,128)S(1)}, f32[8,2048]{1,0:T(8,128)S(1)}, f32[8,128]{1,0:T(8,128)S(1)}) custom-call(s32[2]{0:T(128)S(1)} %bitcast.28, s32[2]{0:T(128)S(1)} %bitcast.29, bf16[704,1024]{1,0:T(8,128)(2,1)} %bitcast.33, bf16[1024,2048]{1,0:T(8,128)(2,1)} %bitcast.31, bf16[2048,1024]{1,0:T(8,128)(2,1)} %bitcast.32, ...), custom_call_target="tpu_custom_call" | custom-call | tf_op jit(solution)/shard_map/summed_grads/pallas_call | solution.py:520
  74.1 0.0 copy-done
  74.1 0.0 copy-done.1
  74.1 0.0 copy-done.2
  74.1 0.0 copy-done.3
  74.1 0.0 copy-done.4
  74.1 0.0 copy-done.5
  74.1 3.0 %clipped_adamw.1 = (f32[1408,256]{1,0:T(8,128)}, f32[1408,256]{1,0:T(8,128)}, f32[1408,256]{1,0:T(8,128)}, f32[8,2048]{1,0:T(8,128)}, f32[8,2048]{1,0:T(8,128)}, /*index=5*/f32[8,2048]{1,0:T(8,128)}) custom-call(f32[8,128]{1,0:T(8,128)S(1)} %get-tuple-element.15.fac, f32[1408,256]{1,0:T(8,128)S(1)} %bitcast.24, f32[1408,256]{1,0:T(8,128)S(1)} %bitcast.21, ...), custom_call_target="tpu_custom_call" | custom-call | tf_op jit(solution)/shard_map/clipped_adamw/pallas_call | solution.py:599
Async XLA Ops:
  0.6 0.7 copy-start.6
  1.3 0.7 copy-start.7
  1.9 72.1 %copy-start = (f32[1,2,704,256]{3,2,1,0:T(8,128)S(1)}, f32[1,2,704,256]{3,2,1,0:T(8,128)}, u32[]{:S(2)}) copy-start(f32[1,2,704,256]{3,2,1,0:T(8,128)} %param.18) | copy-start | bytes 4325380
  2.0 72.1 %copy-start.1 = (f32[1,2,704,256]{3,2,1,0:T(8,128)S(1)}, f32[1,2,704,256]{3,2,1,0:T(8,128)}, u32[]{:S(2)}) copy-start(f32[1,2,704,256]{3,2,1,0:T(8,128)} %param.19) | copy-start | bytes 4325380
  2.0 72.1 %copy-start.2 = (f32[1,2,704,256]{3,2,1,0:T(8,128)S(1)}, f32[1,2,704,256]{3,2,1,0:T(8,128)}, u32[]{:S(2)}) copy-start(f32[1,2,704,256]{3,2,1,0:T(8,128)} %param.20) | copy-start | bytes 4325380
  2.0 72.2 %copy-start.3 = (f32[1,8,2048]{2,1,0:T(8,128)S(1)}, f32[1,8,2048]{2,1,0:T(8,128)}, u32[]{:S(2)}) copy-start(f32[1,8,2048]{2,1,0:T(8,128)} %param.21) | copy-start | bytes 196612
  2.0 72.2 %copy-start.4 = (f32[1,8,2048]{2,1,0:T(8,128)S(1)}, f32[1,8,2048]{2,1,0:T(8,128)}, u32[]{:S(2)}) copy-start(f32[1,8,2048]{2,1,0:T(8,128)} %param.22) | copy-start | bytes 196612
  2.0 72.2 %copy-start.5 = (f32[1,8,2048]{2,1,0:T(8,128)S(1)}, f32[1,8,2048]{2,1,0:T(8,128)}, u32[]{:S(2)}) copy-start(f32[1,8,2048]{2,1,0:T(8,128)} %param.23) | copy-start | bytes 196612

commit v3 on v2

--- a/solution.py
+++ b/solution.py
@@ -11,8 +11,9 @@
 LAYERS = 1
 EXP_DEV = 2
 HALF = FFW // 2
-NCOL = 4
-WCOL = D // NCOL
+WIDTHS = (512, 768, 512, 256)
+NCOL = len(WIDTHS)
+DIRECT = (2, 3)
 
 beta_one = 0.9
 beta_two = 0.95
@@ -107,6 +108,9 @@
     for peer in greeted:
         pl.semaphore_signal(barrier, inc=1, device_id=peer, device_id_type=MESH)
 
+    def cols_of(n):
+        return pl.ds(sum(WIDTHS[:n]), WIDTHS[n])
+
     loads = {}
 
     def load(key, src, dst):
@@ -120,13 +124,14 @@
     load("hid", hid_hbm, hid)
     load_columns(("grd", 2), grd_hbm, grd, (z + 2) % 4 * 512, 512)
     load_columns(("val", 2), val_hbm, val, (y + 2) % 4 * 256, 256)
-    load_columns(("att", 0), att_hbm, att, 0, WCOL)
+    load(("att", 0), att_hbm.at[:, cols_of(0)], att.at[:, cols_of(0)])
     for k in (1, 3, 0):
         load_columns(("val", k), val_hbm, val, (y + k) % 4 * 256, 256)
         load_columns(("grd", k), grd_hbm, grd, (z + k) % 4 * 512, 512)
         if k != 0:
-            load_columns(("att", (k + 1) // 2), att_hbm, att, (k + 1) // 2 * WCOL, WCOL)
-    load_columns(("att", 3), att_hbm, att, 3 * WCOL, WCOL)
+            n = (k + 1) // 2
+            load(("att", n), att_hbm.at[:, cols_of(n)], att.at[:, cols_of(n)])
+    load(("att", 3), att_hbm.at[:, cols_of(3)], att.at[:, cols_of(3)])
     used = set()
 
     def loaded(*keys):
@@ -171,6 +176,10 @@
         for c in held:
             c.start()
         held = None
+
+    def settle():
+        while started:
+            started.pop(0).wait_send()
 
     class Ring:
         def __init__(self, nxt, prv, block, fwd, cmb, direct, add):
@@ -265,9 +274,6 @@
                 part_b[1, c] = prod[:, 256:]
                 go(bx_copy[k])
 
-    def cols_of(n):
-        return pl.ds(n * WCOL, WCOL)
-
     d0_copy = {}
     ring_y, ring_z, dx_copy = [], [], []
     for n in range(NCOL):
@@ -281,25 +287,39 @@
                 y_next,
                 y_prev,
                 lambda k, h, n=n: acc_d.at[(y + k) % 4, h, :, cols_of(n)],
-                lambda d, n=n: fwd_y.at[n, d],
-                lambda d, n=n: cmb_y.at[n, d],
-                lambda d, n=n: dir_y.at[n, d],
+                lambda d, n=n: fwd_y.at[d, :, cols_of(n)],
+                lambda d, n=n: cmb_y.at[d, :, cols_of(n)],
+                lambda d, n=n: dir_y.at[d, :, cols_of(n)],
                 add_f32,
             )
         )
-        ring_z.append(
-            Ring(
-                z_next,
-                z_prev,
-                lambda k, h, n=n: acc_d.at[
-                    y, h, pl.ds(pl.multiple_of((z + k) % 4 * 16, 16), 16), cols_of(n)
-                ],
-                lambda d, n=n: fwd_z.at[n, d],
-                lambda d, n=n: cmb_z.at[n, d],
-                lambda d, n=n: dir_z.at[n, d],
-                add_f32,
+        if n in DIRECT:
+            ring_z.append(
+                [
+                    copy(
+                        acc_d.at[
+                            y, :, pl.ds(pl.multiple_of((z + k) % 4 * 16, 16), 16), cols_of(n)
+                        ],
+                        (fwd_z, cmb_z, dir_z)[k - 1].at[:, :, cols_of(n)],
+                        dev(x, y, (z + k) % 4, core),
+                    )
+                    for k in (1, 2, 3)
+                ]
             )
-        )
+        else:
+            ring_z.append(
+                Ring(
+                    z_next,
+                    z_prev,
+                    lambda k, h, n=n: acc_d.at[
+                        y, h, pl.ds(pl.multiple_of((z + k) % 4 * 16, 16), 16), cols_of(n)
+                    ],
+                    lambda d, n=n: fwd_z.at[d, :, cols_of(n)],
+                    lambda d, n=n: cmb_z.at[d, :, cols_of(n)],
+                    lambda d, n=n: dir_z.at[d, :, cols_of(n)],
+                    add_f32,
+                )
+            )
 
         def x_block(k, n=n):
             t = (x + k) % 4
@@ -307,7 +327,7 @@
             return acc_d.at[y, t % 2, pl.ds(r, 8), cols_of(n)]
 
         dx_copy.append(
-            [copy(x_block(k), recv_dx.at[n, k - 1], dev((x + k) % 4, y, z, core)) for k in (1, 2, 3)]
+            [copy(x_block(k), recv_dx.at[k - 1, :, cols_of(n)], dev((x + k) % 4, y, z, core)) for k in (1, 2, 3)]
         )
 
     def dense_part(k, n):
@@ -315,7 +335,7 @@
         loaded(("val", k), ("att", n))
         lhs = val[:, pl.ds(pl.multiple_of(c * 256, 256), 256)]
         prod = lax.dot_general(lhs, att[:, cols_of(n)], TRANS, preferred_element_type=jnp.float32)
-        part_d[c, :, :, :, cols_of(n)] = prod.reshape(2, 2, 64, WCOL)
+        part_d[c, :, :, :, cols_of(n)] = prod.reshape(2, 2, 64, WIDTHS[n])
         go(d0_copy[k, n])
 
     def dense_core_sum(k, n):
@@ -361,14 +381,26 @@
         for h in (0, 1):
             terms = ring_y[n].terms(h)
             add_f32(terms[0], terms)
+        if n in DIRECT:
+            for k in (1, 0, 2):
+                go(ring_z[n][k])
+            return
         ring_z[n].send_far()
         ring_z[n].send_near(0)
         ring_z[n].send_near(1)
 
     def dense_z_done(n):
-        ring_z[n].wait()
+        if n in DIRECT:
+            for c in ring_z[n]:
+                c.wait_recv()
+        else:
+            ring_z[n].wait()
         for h in (0, 1):
-            terms = ring_z[n].terms(h)
+            if n in DIRECT:
+                mine = acc_d.at[y, h, pl.ds(pl.multiple_of(z * 16, 16), 16), cols_of(n)]
+                terms = [mine] + [b.at[h, :, cols_of(n)] for b in (fwd_z, cmb_z, dir_z)]
+            else:
+                terms = ring_z[n].terms(h)
             add_f32(terms[0], terms)
         for c in dx_copy[n]:
             go(c)
@@ -406,83 +438,82 @@
         r = pl.multiple_of(z * 16 + xh * 8, 8)
         total = acc_d[y, xl, pl.ds(r, 8), cols_of(n)]
         for k in range(3):
-            total = total + recv_dx[n, k]
+            total = total + recv_dx[k, :, cols_of(n)]
         den_out[:, cols_of(n)] = total
         sq = total * total
-        for j in range(WCOL // 128):
+        for j in range(WIDTHS[n] // 128):
             sums["tile"] = sums["tile"] + sq[:, j * 128 : (j + 1) * 128]
 
+    dense_part(2, 0)
     expert_part(2)
+    expert_part(3)
     ring_a.send_far()
+    enter()
+    expert_part(1)
     dense_part(2, 1)
-    dense_part(2, 0)
-    enter()
+    ring_a.send_near(1)
+    dense_core_sum(2, 0)
+    dense_part(1, 0)
+    dense_part(1, 1)
+    ring_a.send_near(0)
+    dense_core_sum(2, 1)
     dense_part(3, 0)
-    expert_part(3)
-    dense_core_sum(2, 1)
-    dense_part(1, 1)
     dense_part(3, 1)
-    dense_core_sum(2, 0)
-    ring_a.send_near(1)
-    dense_part(1, 0)
+    dense_core_sum(3, 0)
+    dense_part(2, 2)
+    dense_part(0, 3)
+    dense_core_sum(1, 1)
+    dense_part(0, 2)
+    dense_core_sum(1, 0)
+    ring_y[0].relay()
+    ring_a.relay()
     dense_core_sum(3, 1)
-    expert_part(1)
-    dense_core_sum(1, 0)
-    dense_part(2, 2)
-    ring_a.send_near(0)
-    dense_core_sum(1, 1)
+    dense_part(3, 2)
+    expert_part(0)
+    dense_part(0, 0)
     dense_part(2, 3)
     dense_part(1, 2)
-    dense_core_sum(3, 0)
-    dense_part(0, 0)
+    dense_core_sum(2, 2)
+    dense_part(0, 1)
     ring_y[1].relay()
     fold_b(2)
+    dense_core_sum(0, 3)
     dense_part(3, 3)
-    ring_a.relay()
-    dense_part(0, 1)
-    dense_part(3, 2)
-    ring_y[0].relay()
+    dense_core_sum(0, 1)
+    dense_core_sum(0, 0)
+    fold_b(3)
+    dense_core_sum(3, 2)
+    dense_y_done(0)
+    dense_core_sum(1, 2)
+    dense_core_sum(2, 3)
     dense_part(1, 3)
-    dense_core_sum(2, 2)
-    dense_core_sum(0, 0)
-    dense_core_sum(1, 2)
     ring_b.send_far()
-    expert_part(0)
+    ring_y[2].relay()
     dense_core_sum(3, 3)
-    dense_core_sum(2, 3)
-    dense_y_done(0)
-    dense_core_sum(3, 2)
-    dense_part(0, 3)
+    ring_z[0].relay()
+    dense_core_sum(0, 2)
+    dense_y_done(1)
     dense_core_sum(1, 3)
     fold_b(1)
-    ring_y[2].relay()
-    dense_part(0, 2)
-    dense_core_sum(0, 1)
+    ring_b.relay()
+    dense_z_done(0)
     expert_a_done()
-    dense_core_sum(0, 2)
-    dense_y_done(1)
-    dense_core_sum(0, 3)
-    fold_b(3)
     ring_y[3].relay()
-    ring_z[0].relay()
-    ring_b.relay()
+    ring_z[1].relay()
+    fold_b(0)
+    dense_last(0)
     dense_y_done(2)
     dense_y_done(3)
-    ring_z[2].relay()
-    ring_z[1].relay()
-    ring_z[3].relay()
     ring_b.send_near(0)
     ring_b.send_near(1)
-    dense_z_done(0)
-    fold_b(0)
+    dense_z_done(1)
     dense_z_done(2)
-    expert_a_last()
-    dense_z_done(1)
     dense_z_done(3)
     dense_last(1)
-    dense_last(0)
+    expert_a_last()
     dense_last(2)
     expert_b_done()
+    settle()
     dense_last(3)
 
     tile = sums["wide"][:, :128] + sums["wide"][:, 128:]
@@ -499,15 +530,13 @@
     n2 = [copy(sq_row, recv_n2.at[k], ep_peers[k]) for k in range(15)]
     for c in n2:
         go(c)
+    settle()
     for k, c in enumerate(n2):
         c.wait_recv()
         tile = tile + recv_n2[k]
     norm = jnp.sqrt(jnp.sum(tile, axis=1, keepdims=True))
     factor = jnp.minimum(1.0, jnp.sqrt(jnp.full((1, 1), total_count, jnp.float32)) / (norm + 1e-06))
     fac_out[...] = jnp.broadcast_to(factor, (8, 128))
-
-    for c in started:
-        c.wait_send()
 
 
 def summed_grads(hid_t, grd, counts, offsets, val, att, total_count):
@@ -546,13 +575,13 @@
             vm((2, HALF, 256), bf),
             vm((4, 2, 2, 64, D), f32),
             vm((4, 2, 64, D), f32),
-            vm((NCOL, 2, 64, WCOL), f32),
-            vm((NCOL, 2, 64, WCOL), f32),
-            vm((NCOL, 2, 64, WCOL), f32),
-            vm((NCOL, 2, 16, WCOL), f32),
-            vm((NCOL, 2, 16, WCOL), f32),
-            vm((NCOL, 2, 16, WCOL), f32),
-            vm((NCOL, 3, 8, WCOL), f32),
+            vm((2, 64, D), f32),
+            vm((2, 64, D), f32),
+            vm((2, 64, D), f32),
+            vm((2, 16, D), f32),
+            vm((2, 16, D), f32),
+            vm((2, 16, D), f32),
+            vm((3, 8, D), f32),
             vm((1, 128), f32),
             vm((1, 128), f32),
             vm((7, 1, 128), f32),

time: 77.5 us -> 76.6 us (0.988)
  Pallas kernels: 75.1 us -> 74.3 us
    pallas_call x1, Pallas kernels: 72.1 us -> 71.3 us  [summed_grads(): pl.pallas_call(lambda *refs: grad_kernel(total_count, *refs), name='summe...]
where the time goes in v3:
time: 76.6 us; the launch traced here: 76.5 us
  Pallas kernels  74.3 us (97%)
  local copies, waits for them, and re-layouts  1.33 us (2%)
  between operations  0.9 us (1%)
    pallas_call x1, Pallas kernels, summed_grads(): pl.pallas_call(lambda *refs: grad_kernel(total_count, *refs), name='summe...  71.3 us
    pallas_call x1, Pallas kernels, updated(): pl.pallas_call(adam_kernel, name='clipped_adamw', out_shape=[jax.ShapeDty...  3.01 us

profile of v3, /device:TPU:1, one launch (start us, length us, event | category | flops | bytes accessed | tf_op | source)
XLA Modules:
  0.0 76.5 jit_solution(18246734453983910193)
XLA Ops:
  0.6 0.0 copy-start.6
  0.6 0.6 copy-done.6
  1.3 0.0 copy-start.7
  1.3 0.7 copy-done.7
  1.9 0.0 copy-start
  2.0 0.0 copy-start.1
  2.0 0.0 copy-start.2
  2.0 0.0 copy-start.3
  2.0 0.0 copy-start.4
  2.0 0.0 copy-start.5
  2.0 71.3 %summed_grads.1 = (f32[2,704,256]{2,1,0:T(8,128)S(1)}, f32[8,2048]{1,0:T(8,128)S(1)}, f32[8,128]{1,0:T(8,128)S(1)}) custom-call(s32[2]{0:T(128)S(1)} %bitcast.28, s32[2]{0:T(128)S(1)} %bitcast.29, bf16[704,1024]{1,0:T(8,128)(2,1)} %bitcast.33, bf16[1024,2048]{1,0:T(8,128)(2,1)} %bitcast.31, bf16[2048,1024]{1,0:T(8,128)(2,1)} %bitcast.32, ...), custom_call_target="tpu_custom_call" | custom-call | tf_op jit(solution)/shard_map/summed_grads/pallas_call | solution.py:549
  73.2 0.0 copy-done
  73.3 0.0 copy-done.1
  73.3 0.0 copy-done.2
  73.3 0.0 copy-done.3
  73.3 0.0 copy-done.4
  73.3 0.0 copy-done.5
  73.3 3.0 %clipped_adamw.1 = (f32[1408,256]{1,0:T(8,128)}, f32[1408,256]{1,0:T(8,128)}, f32[1408,256]{1,0:T(8,128)}, f32[8,2048]{1,0:T(8,128)}, f32[8,2048]{1,0:T(8,128)}, /*index=5*/f32[8,2048]{1,0:T(8,128)}) custom-call(f32[8,128]{1,0:T(8,128)S(1)} %get-tuple-element.15.fac, f32[1408,256]{1,0:T(8,128)S(1)} %bitcast.24, f32[1408,256]{1,0:T(8,128)S(1)} %bitcast.21, ...), custom_call_target="tpu_custom_call" | custom-call | tf_op jit(solution)/shard_map/clipped_adamw/pallas_call | solution.py:628
Async XLA Ops:
  0.6 0.7 copy-start.6
  1.3 0.7 copy-start.7
  1.9 71.3 %copy-start = (f32[1,2,704,256]{3,2,1,0:T(8,128)S(1)}, f32[1,2,704,256]{3,2,1,0:T(8,128)}, u32[]{:S(2)}) copy-start(f32[1,2,704,256]{3,2,1,0:T(8,128)} %param.18) | copy-start | bytes 4325380
  2.0 71.3 %copy-start.1 = (f32[1,2,704,256]{3,2,1,0:T(8,128)S(1)}, f32[1,2,704,256]{3,2,1,0:T(8,128)}, u32[]{:S(2)}) copy-start(f32[1,2,704,256]{3,2,1,0:T(8,128)} %param.19) | copy-start | bytes 4325380
  2.0 71.3 %copy-start.2 = (f32[1,2,704,256]{3,2,1,0:T(8,128)S(1)}, f32[1,2,704,256]{3,2,1,0:T(8,128)}, u32[]{:S(2)}) copy-start(f32[1,2,704,256]{3,2,1,0:T(8,128)} %param.20) | copy-start | bytes 4325380
  2.0 71.3 %copy-start.3 = (f32[1,8,2048]{2,1,0:T(8,128)S(1)}, f32[1,8,2048]{2,1,0:T(8,128)}, u32[]{:S(2)}) copy-start(f32[1,8,2048]{2,1,0:T(8,128)} %param.21) | copy-start | bytes 196612
  2.0 71.3 %copy-start.4 = (f32[1,8,2048]{2,1,0:T(8,128)S(1)}, f32[1,8,2048]{2,1,0:T(8,128)}, u32[]{:S(2)}) copy-start(f32[1,8,2048]{2,1,0:T(8,128)} %param.22) | copy-start | bytes 196612
  2.0 71.3 %copy-start.5 = (f32[1,8,2048]{2,1,0:T(8,128)S(1)}, f32[1,8,2048]{2,1,0:T(8,128)}, u32[]{:S(2)}) copy-start(f32[1,8,2048]{2,1,0:T(8,128)} %param.23) | copy-start | bytes 196612

commit v4 on v3

--- a/solution.py
+++ b/solution.py
@@ -40,8 +40,7 @@
 
 def grad_kernel(
     total_count,
-    counts,
-    offsets,
+    segments,
     hid_hbm,
     grd_hbm,
     val_hbm,
@@ -143,8 +142,8 @@
     loaded("hid")
     lane = lax.broadcasted_iota(jnp.int32, (FFW, 1024), 1)
     for e in range(EXP_DEV):
-        rel = lane - offsets[e]
-        keep = jnp.logical_and(rel >= 0, rel < counts[e])
+        rel = lane - segments[EXP_DEV + e]
+        keep = jnp.logical_and(rel >= 0, rel < segments[e])
         hmask[e] = jnp.where(keep, hid[...], jnp.zeros_like(hid))
 
     started = []
@@ -539,7 +538,7 @@
     fac_out[...] = jnp.broadcast_to(factor, (8, 128))
 
 
-def summed_grads(hid_t, grd, counts, offsets, val, att, total_count):
+def summed_grads(hid_t, grd, segments, val, att, total_count):
     vm = pltpu.VMEM
     bf = jnp.bfloat16
     f32 = jnp.float32
@@ -554,7 +553,7 @@
             jax.ShapeDtypeStruct((8, D), f32),
             jax.ShapeDtypeStruct((8, 128), f32),
         ),
-        in_specs=[smem, smem, hbm, hbm, hbm, hbm],
+        in_specs=[smem, hbm, hbm, hbm, hbm],
         out_specs=(vmem, vmem, vmem),
         scratch_shapes=[
             vm((FFW, 1024), bf),
@@ -593,7 +592,7 @@
         compiler_params=pltpu.CompilerParams(
             collective_id=0, has_side_effects=True, vmem_limit_bytes=52 << 20
         ),
-    )(counts, offsets, hid_t, grd, val, att)
+    )(segments, hid_t, grd, val, att)
 
 
 STEPS = 11
@@ -657,8 +656,7 @@
     expert_total, dense_total, factor = summed_grads(
         routed_hidden[0, 0].T,
         routed_grads[0, 0],
-        expert_counts[0, 0],
-        expert_offsets[0, 0],
+        jnp.concatenate([expert_counts[0, 0], expert_offsets[0, 0]]),
         attn_values[0],
         attn_grads[0],
         total_count,

time: 76.6 us -> 76.1 us (level)
  local copies, waits for them, and re-layouts: 1.33 us -> 0.03 us
    unnamed x16 -> x12, local copies, waits for them, and re-layouts: 1.33 us -> 0.03 us
where the time goes in v4:
time: 76.1 us; the launch traced here: 75.9 us
  Pallas kernels  74.3 us (98%)
  between operations  0.89 us (1%)
    pallas_call x1, Pallas kernels, summed_grads(): pl.pallas_call(lambda *refs: grad_kernel(total_count, *refs), name='summe...  71.3 us
    pallas_call x1, Pallas kernels, updated(): pl.pallas_call(adam_kernel, name='clipped_adamw', out_shape=[jax.ShapeDty...  3.01 us

profile of v4, /device:TPU:1, one launch (start us, length us, event | category | flops | bytes accessed | tf_op | source)
XLA Modules:
  0.0 75.9 jit_solution(16151152278922745317)
XLA Ops:
  0.6 0.7 pad_add_fusion.refs_0_
  1.4 0.0 copy-start
  1.4 0.0 copy-start.1
  1.4 0.0 copy-start.2
  1.4 0.0 copy-start.3
  1.4 0.0 copy-start.4
  1.4 0.0 copy-start.5
  1.4 71.3 %summed_grads.1 = (f32[2,704,256]{2,1,0:T(8,128)S(1)}, f32[8,2048]{1,0:T(8,128)S(1)}, f32[8,128]{1,0:T(8,128)S(1)}) custom-call(s32[4]{0:T(128)S(1)} %pad_add_fusion.refs_0_, bf16[704,1024]{1,0:T(8,128)(2,1)} %bitcast.31, bf16[1024,2048]{1,0:T(8,128)(2,1)} %bitcast.29, bf16[2048,1024]{1,0:T(8,128)(2,1)} %bitcast.30, bf16[2048,2048]{1,0:T(8,128)(2,1)} %bitcast.28), custom_call_target="tpu_custom_call" | custom-call | tf_op jit(solution)/shard_map/summed_grads/pallas_call | solution.py:548
  72.7 0.0 copy-done
  72.7 0.0 copy-done.1
  72.7 0.0 copy-done.2
  72.7 0.0 copy-done.3
  72.7 0.0 copy-done.4
  72.7 0.0 copy-done.5
  72.7 3.0 %clipped_adamw.1 = (f32[1408,256]{1,0:T(8,128)}, f32[1408,256]{1,0:T(8,128)}, f32[1408,256]{1,0:T(8,128)}, f32[8,2048]{1,0:T(8,128)}, f32[8,2048]{1,0:T(8,128)}, /*index=5*/f32[8,2048]{1,0:T(8,128)}) custom-call(f32[8,128]{1,0:T(8,128)S(1)} %get-tuple-element.15.fac, f32[1408,256]{1,0:T(8,128)S(1)} %bitcast.24, f32[1408,256]{1,0:T(8,128)S(1)} %bitcast.21, ...), custom_call_target="tpu_custom_call" | custom-call | tf_op jit(solution)/shard_map/clipped_adamw/pallas_call | solution.py:627
Async XLA Ops:
  1.4 71.3 %copy-start = (f32[1,2,704,256]{3,2,1,0:T(8,128)S(1)}, f32[1,2,704,256]{3,2,1,0:T(8,128)}, u32[]{:S(2)}) copy-start(f32[1,2,704,256]{3,2,1,0:T(8,128)} %param.18) | copy-start | bytes 4325380
  1.4 71.3 %copy-start.1 = (f32[1,2,704,256]{3,2,1,0:T(8,128)S(1)}, f32[1,2,704,256]{3,2,1,0:T(8,128)}, u32[]{:S(2)}) copy-start(f32[1,2,704,256]{3,2,1,0:T(8,128)} %param.19) | copy-start | bytes 4325380
  1.4 71.3 %copy-start.2 = (f32[1,2,704,256]{3,2,1,0:T(8,128)S(1)}, f32[1,2,704,256]{3,2,1,0:T(8,128)}, u32[]{:S(2)}) copy-start(f32[1,2,704,256]{3,2,1,0:T(8,128)} %param.20) | copy-start | bytes 4325380
  1.4 71.3 %copy-start.3 = (f32[1,8,2048]{2,1,0:T(8,128)S(1)}, f32[1,8,2048]{2,1,0:T(8,128)}, u32[]{:S(2)}) copy-start(f32[1,8,2048]{2,1,0:T(8,128)} %param.21) | copy-start | bytes 196612
  1.4 71.3 %copy-start.4 = (f32[1,8,2048]{2,1,0:T(8,128)S(1)}, f32[1,8,2048]{2,1,0:T(8,128)}, u32[]{:S(2)}) copy-start(f32[1,8,2048]{2,1,0:T(8,128)} %param.22) | copy-start | bytes 196612
  1.4 71.3 %copy-start.5 = (f32[1,8,2048]{2,1,0:T(8,128)S(1)}, f32[1,8,2048]{2,1,0:T(8,128)}, u32[]{:S(2)}) copy-start(f32[1,8,2048]{2,1,0:T(8,128)} %param.23) | copy-start | bytes 196612
